TPU v7x, 32 devices: a whole 2x2x4 slice. The times are simulated.
32 devices in a mesh: lon: 16 (over z, y, core), lat: 2 (over x).
Axes of the slice: x: 2, y: 2, z: 4, core: 2. Of those that a mesh axis runs over, the one named last changes fastest.
Arguments:
- field: bfloat16 [1, 64, 256, 256], P(None, 'lat', 'lon'), may hold values from -6 to 6
- depth_kernel: float32 [7, 7, 256], replicated, may hold values from -0.875 to 0.875
- layer_norm_gain: float32 [256], replicated, may hold values from 0.1 to 1.9
- inner_weight: bfloat16 [256, 1024], replicated, may hold values from -0.375 to 0.375
- outer_weight: bfloat16 [1024, 256], replicated, may hold values from -0.1875 to 0.1875
- layer_scale: float32 [256], replicated, may hold values from 0.3 to 1.5
- down_weight: bfloat16 [1024, 512], replicated, may hold values from -0.1875 to 0.1875
- cotangent: bfloat16 [1, 32, 128, 512], P(None, 'lat', 'lon'), may hold values from -6 to 6
Outputs:
- coarse: bfloat16 [1, 32, 128, 512], P(None, 'lat', 'lon')
- grad_field: bfloat16 [1, 64, 256, 256], P(None, 'lat', 'lon')
- grad_kernel: float32 [7, 7, 256], replicated
- grad_gain: float32 [256], replicated
- grad_inner: float32 [256, 1024], replicated
- grad_outer: float32 [1024, 256], replicated
- grad_scale: float32 [256], replicated
- grad_down: float32 [1024, 512], replicated
All inputs are finite; a program needn't handle non-finite values.
Results may differ from a plain program's by a relative error of at most 0.0071.
Values may be sent and summed in bfloat16 or wider, within the bound.
A program may use at most 64 MiB of HBM per device.

v0:
```python
from functools import partial
import math
import jax
import jax.numpy as jnp
from jax import lax
from jax.sharding import PartitionSpec as P

PARAMS = 1061632
EPS = 1e-06


def padded_2(cells, sides, width, closed):
    for axis, dim in sides:
        count = lax.axis_size(axis)
        ends = count if closed else count - 1
        head = lax.slice_in_dim(cells, 0, width, axis=dim)
        tail = lax.slice_in_dim(cells, cells.shape[dim] - width, cells.shape[dim], axis=dim)
        cells = jnp.concatenate(
            [
                lax.ppermute(tail, axis, [(i, (i + 1) % count) for i in range(ends)]),
                cells,
                lax.ppermute(head, axis, [((i + 1) % count, i) for i in range(ends)]),
            ],
            axis=dim,
        )
    return cells


def depth_apply(padded, kernel):
    rows = padded.shape[1] - 6
    cols = padded.shape[2] - 6
    total = jnp.zeros((padded.shape[0], rows, cols, padded.shape[3]), jnp.float32)
    for row_shift in range(7):
        for col_shift in range(7):
            total = (
                total
                + kernel[row_shift, col_shift]
                * padded[:, row_shift : row_shift + rows, col_shift : col_shift + cols]
            )
    return total


def depth_transpose(padded, kernel):
    rows = padded.shape[1] - 6
    cols = padded.shape[2] - 6
    total = jnp.zeros((padded.shape[0], rows, cols, padded.shape[3]), jnp.float32)
    for row_shift in range(7):
        for col_shift in range(7):
            total = (
                total
                + kernel[row_shift, col_shift]
                * padded[
                    :, 6 - row_shift : 6 - row_shift + rows, 6 - col_shift : 6 - col_shift + cols
                ]
            )
    return total


def kernel_terms(padded, grad):
    rows = grad.shape[1]
    cols = grad.shape[2]
    terms = []
    for row_shift in range(7):
        for col_shift in range(7):
            terms.append(
                jnp.sum(
                    padded[:, row_shift : row_shift + rows, col_shift : col_shift + cols] * grad,
                    axis=(0, 1, 2),
                )
            )
    return jnp.stack(terms).reshape(7, 7, grad.shape[3])


def to_patches(values):
    batch, rows, cols, channel_count = values.shape
    return (
        values.reshape(batch, rows // 2, 2, cols // 2, 2, channel_count)
        .transpose(0, 1, 3, 2, 4, 5)
        .reshape(-1, 4 * channel_count)
    )


def from_patches(values, shape):
    batch, rows, cols, channel_count = shape
    return (
        values.reshape(batch, rows // 2, cols // 2, 2, 2, channel_count)
        .transpose(0, 1, 3, 2, 4, 5)
        .reshape(batch, rows, cols, channel_count)
    )


def reduce_down(raw_down):
    return lax.psum(raw_down, ("lon", "lat"))


def body(
    field,
    depth_kernel,
    layer_norm_gain,
    inner_weight,
    outer_weight,
    layer_scale,
    down_weight,
    cotangent,
):
    channel_count = field.shape[3]
    wide = padded_2(field, (("lon", 2),), 3, True)
    padded = padded_2(wide, (("lat", 1),), 3, False)
    mixed = depth_apply(padded.astype(jnp.float32), depth_kernel)
    centered_input = mixed - jnp.mean(mixed, axis=-1, keepdims=True)
    inverse_deviation = lax.rsqrt(
        jnp.mean(centered_input * centered_input, axis=-1, keepdims=True) + EPS
    )
    standardized_input = centered_input * inverse_deviation
    normalized_output = (
        (standardized_input * layer_norm_gain).astype(jnp.bfloat16).reshape(-1, channel_count)
    )
    preact = jnp.dot(normalized_output, inner_weight, preferred_element_type=jnp.float32)
    hidden = jax.nn.gelu(preact, approximate=False).astype(jnp.bfloat16)
    branch = jnp.dot(hidden, outer_weight, preferred_element_type=jnp.float32)
    blocked = (field.astype(jnp.float32).reshape(-1, channel_count) + layer_scale * branch).astype(
        jnp.bfloat16
    )
    patches = to_patches(blocked.reshape(field.shape))
    coarse = jnp.dot(patches, down_weight, preferred_element_type=jnp.float32).astype(jnp.bfloat16)
    coarse = coarse.reshape(cotangent.shape)
    flat_grad = cotangent.reshape(-1, cotangent.shape[3])
    raw_down = jnp.dot(patches.T, flat_grad, preferred_element_type=jnp.float32)
    grad_patch = jnp.dot(flat_grad, down_weight.T, preferred_element_type=jnp.float32).astype(
        jnp.bfloat16
    )
    grad_blocked = from_patches(grad_patch, field.shape).reshape(-1, channel_count)
    raw_scale = jnp.sum(grad_blocked.astype(jnp.float32) * branch, axis=0)
    grad_branch = (grad_blocked.astype(jnp.float32) * layer_scale).astype(jnp.bfloat16)
    grad_hidden = jnp.dot(grad_branch, outer_weight.T, preferred_element_type=jnp.float32)
    grad_pre = jax.vjp(partial(jax.nn.gelu, approximate=False), preact)[1](grad_hidden)[0].astype(
        jnp.bfloat16
    )
    raw_outer = jnp.dot(hidden.T, grad_branch, preferred_element_type=jnp.float32)
    raw_inner = jnp.dot(normalized_output.T, grad_pre, preferred_element_type=jnp.float32)
    normalized_gradient = jnp.dot(
        grad_pre, inner_weight.T, preferred_element_type=jnp.float32
    ).reshape(mixed.shape)
    unclipped_gain = jnp.sum(normalized_gradient * standardized_input, axis=(0, 1, 2))
    gain_scaled_output = normalized_gradient * layer_norm_gain
    depthwise_gradient = (
        gain_scaled_output
        - jnp.mean(gain_scaled_output, axis=-1, keepdims=True)
        - standardized_input
        * jnp.mean(gain_scaled_output * standardized_input, axis=-1, keepdims=True)
    ) * inverse_deviation
    depthwise_gradient = depthwise_gradient.astype(jnp.bfloat16)
    grad_wide = padded_2(depthwise_gradient, (("lon", 2),), 3, True)
    grad_padded = padded_2(grad_wide, (("lat", 1),), 3, False).astype(jnp.float32)
    spread = depth_transpose(grad_padded, depth_kernel)
    grad_field = (grad_blocked.reshape(field.shape).astype(jnp.float32) + spread).astype(
        jnp.bfloat16
    )
    raw_kernel = kernel_terms(padded.astype(jnp.float32), depthwise_gradient.astype(jnp.float32))
    summed_down = reduce_down(raw_down)
    limit = math.sqrt(PARAMS)
    sum_kernel, sum_gain, sum_inner, sum_outer, sum_scale = lax.psum(
        (raw_kernel, unclipped_gain, raw_inner, raw_outer, raw_scale), ("lon", "lat")
    )
    total = (
        jnp.sum(sum_kernel * sum_kernel)
        + jnp.sum(sum_gain * sum_gain)
        + jnp.sum(sum_inner * sum_inner)
        + jnp.sum(sum_outer * sum_outer)
        + jnp.sum(sum_scale * sum_scale)
        + jnp.sum(summed_down * summed_down)
    )
    factor = jnp.minimum(1.0, limit / jnp.sqrt(total + EPS))
    grad_kernel = sum_kernel * factor
    grad_gain = sum_gain * factor
    grad_inner = sum_inner * factor
    grad_outer = sum_outer * factor
    grad_scale = sum_scale * factor
    grad_down = summed_down * factor
    return (
        coarse,
        grad_field,
        grad_kernel,
        grad_gain,
        grad_inner,
        grad_outer,
        grad_scale,
        grad_down,
    )


def solution(mesh):
    return jax.shard_map(
        body,
        mesh=mesh,
        in_specs=(
            P(None, "lat", "lon", None),
            P(),
            P(),
            P(),
            P(),
            P(),
            P(),
            P(None, "lat", "lon", None),
        ),
        out_specs=(
            P(None, "lat", "lon", None),
            P(None, "lat", "lon", None),
            P(),
            P(),
            P(),
            P(),
            P(),
            P(),
        ),
        check_vma=False,
    )
```

profile of v0, /device:TPU:0, one launch (start us, length us, event | category | flops | bytes accessed | tf_op | source)
XLA Modules:
  0.0 220.6 jit_solution(751683770909935926)
XLA Ops:
  7.2 0.0 copy-start
  7.2 0.0 all-reduce.4.cloned.1.call-start
  7.2 1.1 fusion.114
  8.3 0.5 collective-permute-start
  8.8 5.1 %collective-permute-start.1 = (bf16[1,32,3,256]{3,2,1,0:T(4,128)(2,1)S(1)}, bf16[1,32,3,256]{3,2,1,0:T(4,128)(2,1)S(1)}, u32[]{:S(2)}, u32[]{:S(2)}) collective-permute-start(bf16[1,32,3,256]{3,2,1,0:T(4,128)(2,1)S(1)} %get-tuple-element.79), channel_id=1, source_target_pairs={{2,0},{4,2},{6,4},{8,6},{10,8},{12,10},{14,12},{16,14},{18,16},{20... | collective-permute-start | bytes 147464 | tf_op jit(solution)/shard_map/ppermute | solution.py:22
  13.9 1.0 fusion.115
  15.1 1.4 convolution_convert_fusion
  16.5 1.0 fusion.116
  17.8 0.8 pad_maximum_fusion.5
  18.6 3.8 %collective-permute-start.2 = (bf16[1,3,22,256]{3,2,1,0:T(8,128)(2,1)S(1)}, bf16[1,3,22,256]{3,2,1,0:T(8,128)(2,1)S(1)}, u32[]{:S(2)}, u32[]{:S(2)}) collective-permute-start(bf16[1,3,22,256]{3,2,1,0:T(8,128)(2,1)S(1)} %get-tuple-element.74), channel_id=1, source_target_pairs={{0,1},{2,3},{4,5},{6,7},{8,9},{10,11},{12,13},{14,15},{16,17},{18,... | collective-permute-start | bytes 101384 | tf_op jit(solution)/shard_map/ppermute | solution.py:20
  22.4 1.3 collective-permute-start.3
  23.7 1.5 fusion.117
  25.2 0.2 copy.21
  25.4 0.4 reshape.367
  25.8 1.2 reshape.366
  26.9 1.3 collective-permute-done.3
  28.2 0.2 maximum_convert_fusion
  28.8 0.0 copy-start.98
  28.8 4.5 %fusion.112 = (f32[32,16]{1,0:T(8,128)S(1)}, f32[1,32,16,256]{3,2,1,0:T(8,128)S(1)}) fusion(f32[1,38,22,256]{3,2,1,0:T(8,128)S(1)} %maximum_convert_fusion, f32[256]{0:T(256)} %bitcast.49, f32[256]{0:T(256)} %bitcast.48, f32[256]{0:T(256)S(1)} %bitcast.144, f32[256]{0:T(256)S(1)} %bitcast.146, f32[256]{0:T(256)S(1)} %bitcast.148, f32[256]{0:T(256)S(1)} %bitcast.150, ...), kind=kLoop, calls=%fused_computation.259 | loop fusion | flops 12844544 | bytes 26266624 | tf_op jit(solution)/shard_map/reduce_sum | solution.py:110
  33.4 0.2 multiply_reduce_fusion.7
  33.7 0.2 multiply_convert_fusion.3
  33.9 0.1 copy-done.10
  34.0 0.3 copy-done.11
  34.3 5.8 %multiply_convert_fusion = (bf16[512,1024]{1,0:T(8,128)(2,1)S(1)}, f32[512,1024]{1,0:T(8,128)S(1)}, f32[512,1024]{1,0:T(8,128)S(1)}) fusion(bf16[512,256]{1,0:T(8,128)(2,1)S(1)} %bitcast.138, bf16[256,1024]{1,0:T(8,128)(2,1)S(1)} %copy-done.98), kind=kOutput, calls=%fused_computation.53 | convolution fusion | flops 302514176 | bytes 6029312 | tf_op jit(solution)/shard_map/dot_general | solution.py:118
  40.1 1.5 fusion.110
  41.6 1.0 multiply_reduce_fusion.3
  42.6 1.0 add_convert_fusion
  43.6 1.1 multiply_reduce_fusion.6
  44.8 1.4 fusion.118
  46.2 0.1 reshape_reshape.4
  46.3 0.9 copy.22
  47.2 1.1 reshape.359
  48.4 0.7 broadcast_multiply_fusion.6
  49.0 0.7 div.20
  49.7 1.6 multiply_reduce_fusion.4
  51.3 3.0 %fusion.54 = (f32[256]{0:T(256)}, f32[256]{0:T(256)}, f32[256]{0:T(256)}, f32[256]{0:T(256)}, f32[256]{0:T(256)}, /*index=5*/f32[256]{0:T(256)}, f32[256]{0:T(25...) fusion(f32[1,38,22,256]{3,2,1,0:T(8,128)S(1)} %maximum_convert_, ...), kind=kLoop, calls=%fused_computation.120 | loop fusion | flops 5893632 | bytes 10775552 | tf_op jit(solution)/shard_map/reduce_sum | solution.py:66
  54.3 1.1 fusion.55
  55.4 1.8 fusion.107
  57.2 0.0 all-reduce.4.cloned.1.call-update
  57.2 0.7 fusion.53
  58.3 2.9 %stack.199 = f32[49,256]{1,0:T(8,128)S(1)} concatenate(f32[1,256]{1,0:T(1,128)S(1)} %bitcast.250, f32[1,256]{1,0:T(1,128)S(1)} %bitcast.252, f32[1,256]{1,0:T(1,128)S(1)} %bitcast.253, f32[1,256]{1,0:T(1,128)S(1)} %bitcast.254, f32[1,256]{1,0:T(1,128)S(1)} %bitcast.255, f32[1,256]{1,0:T(1,128)S(1)} %bitcast.256, f32[1,256]{1,0:T(1,128)S(1)} %bitcast.257, f32[1,256]{1,0:T(1,128)S(1)} %bitcast.258, ...), dimensions={0} | concatenate | bytes 100352 | tf_op jit(solution)/shard_map/stack | solution.py:71
  61.2 0.1 fusion.113
  61.3 0.1 collective-permute-start.4
  61.4 4.4 %collective-permute-start.5 = (bf16[1,32,3,256]{3,2,1,0:T(4,128)(2,1)S(1)}, bf16[1,32,3,256]{3,2,1,0:T(4,128)(2,1)S(1)}, u32[]{:S(2)}, u32[]{:S(2)}) collective-permute-start(bf16[1,32,3,256]{3,2,1,0:T(4,128)(2,1)S(1)} %get-tuple-element.77), channel_id=1, source_target_pairs={{2,0},{4,2},{6,4},{8,6},{10,8},{12,10},{14,12},{16,14},{18,16},{20... | collective-permute-start | bytes 147464 | tf_op jit(solution)/shard_map/ppermute | solution.py:22
  65.8 38.1 %all-reduce = (f32[7,7,256]{2,1,0:T(8,128)S(1)}, f32[256]{0:T(256)S(1)}, f32[256]{0:T(256)S(1)}) all-reduce(f32[7,7,256]{2,1,0:T(8,128)S(1)} %reshape.363, f32[256]{0:T(256)} %get-tuple-element.57, f32[256]{0:T(256)} %get-tuple-element.70), channel_id=1, replica_groups=mesh['lon'=16,'lat'=2] {'lon','lat'}, use_global_device_ids=true, to_apply=%region_53.0 | all-reduce | flops 13056 | bytes 104448 | tf_op jit(solution)/shard_map/psum | solution.py:162
  104.0 1.0 fusion.6
  105.0 0.6 multiply_reduce_fusion.8
  105.6 4.2 %collective-permute-start.6 = (bf16[1,3,22,256]{3,2,1,0:T(8,128)(2,1)S(1)}, bf16[1,3,22,256]{3,2,1,0:T(8,128)(2,1)S(1)}, u32[]{:S(2)}, u32[]{:S(2)}) collective-permute-start(bf16[1,3,22,256]{3,2,1,0:T(8,128)(2,1)S(1)} %get-tuple-element.72), channel_id=1, source_target_pairs={{0,1},{2,3},{4,5},{6,7},{8,9},{10,11},{12,13},{14,15},{16,17},{18,... | collective-permute-start | bytes 101384 | tf_op jit(solution)/shard_map/ppermute | solution.py:20
  109.8 1.3 collective-permute-start.7
  111.1 0.7 multiply_reduce_fusion.9
  113.0 2.6 %collective-permute-done.7 = bf16[1,3,22,256]{3,2,1,0:T(8,128)(2,1)S(1)} collective-permute-done((bf16[1,3,22,256]{3,2,1,0:T(8,128)(2,1)S(1)}, bf16[1,3,22,256]{3,2,1,0:T(8,128)(2,1)S(1)}, u32[]{:S(2)}, u32[]{:S(2)}) %collective-permute-start.7) | collective-permute-done | bytes 33824 | tf_op jit(solution)/shard_map/ppermute | solution.py:22
  115.6 0.2 maximum_convert_fusion.1
  116.2 5.1 %fusion.58 = bf16[1,32,16,256]{3,2,1,0:T(8,128)(2,1)} fusion(f32[1,32,16,256]{3,2,1,0:T(8,128)S(1)} %copy-done.7, f32[1,38,22,256]{3,2,1,0:T(8,128)S(1)} %maximum_convert_fusion.1, f32[256]{0:T(256)} %bitcast.49, f32[256]{0:T(256)} %bitcast.48, f32[256]{0:T(256)S(1)} %bitcast.145, f32[256]{0:T(256)S(1)} %bitcast.147, f32[256]{0:T(256)S(1)} %bitcast.149, ...), kind=kLoop, calls=%fused_computation.125 | loop fusion | flops 12976128 | bytes 26526720 | tf_op jit(solution)/shard_map/convert_element_type | solution.py:156
  121.3 79.2 %all-reduce.4.cloned.1.call-done = (f32[256,1024]{1,0:T(8,128)}, f32[1024,256]{1,0:T(8,128)}, f32[1024,512]{1,0:T(8,128)}) async-done(((f32[256,1024]{1,0:T(8,128)}, f32[1024,256]{1,0:T(8,128)}, f32[1024,512]{1,0:T(8,128)}), (f32[256,1024]{1,0:T(8,128)}, f32[1024,256]{1,0:T(8,128)}, f32[1024,512]{1,0:T(8,128)})) %all-reduce.4.cloned.1.call-update) | async-done | bytes 4194320 | tf_op jit(solution)/shard_map/psum | solution.py:162
  200.5 2.9 %multiply_reduce_fusion = f32[]{:T(128)} fusion(f32[1024,512]{1,0:T(8,128)} %get-tuple-element.64), kind=kLoop, calls=%fused_computation.51 | loop fusion | flops 1048575 | bytes 2097156 | tf_op jit(solution)/shard_map/reduce_sum | solution.py:171
  203.3 0.9 multiply_reduce_fusion.1
  204.2 0.9 multiply_reduce_fusion.2
  207.8 0.6 broadcast_multiply_fusion.7
  208.3 1.5 broadcast_multiply_fusion
  209.9 1.0 broadcast_multiply_fusion.1
  210.9 0.6 copy-done.3
  211.5 1.1 broadcast_multiply_fusion.2
  212.6 0.6 broadcast_multiply_fusion.8
  213.1 0.6 broadcast_multiply_fusion.3
  (204 shorter events, 0.5 us)
Async XLA Ops:
  7.2 193.3 %all-reduce.4.cloned.1.call-start = ((), (), s32[]{:S(2)}) async-start(), calls=%async_computation | async-start | bytes 8388608 | tf_op jit(solution)/shard_map/psum | solution.py:162
  8.3 9.4 %collective-permute-start = (bf16[1,32,3,256]{3,2,1,0:T(4,128)(2,1)S(1)}, bf16[1,32,3,256]{3,2,1,0:T(4,128)(2,1)S(1)}, u32[]{:S(2)}, u32[]{:S(2)}) collective-permute-start(bf16[1,32,3,256]{3,2,1,0:T(4,128)(2,1)S(1)} %get-tuple-element.78), channel_id=1, source_target_pairs={{0,2},{2,4},{4,6},{6,8},{8,10},{10,12},{12,14},{14,16},{16,18},{18... | collective-permute-start | bytes 147464 | tf_op jit(solution)/shard_map/ppermute | solution.py:20
  8.8 8.9 %collective-permute-start.1 = (bf16[1,32,3,256]{3,2,1,0:T(4,128)(2,1)S(1)}, bf16[1,32,3,256]{3,2,1,0:T(4,128)(2,1)S(1)}, u32[]{:S(2)}, u32[]{:S(2)}) collective-permute-start(bf16[1,32,3,256]{3,2,1,0:T(4,128)(2,1)S(1)} %get-tuple-element.79), channel_id=1, source_target_pairs={{2,0},{4,2},{6,4},{8,6},{10,8},{12,10},{14,12},{16,14},{18,16},{20... | collective-permute-start | bytes 147464 | tf_op jit(solution)/shard_map/ppermute | solution.py:22
  14.9 13.5 %copy-start.15 = (f32[1,1,256]{2,1,0:T(1,128)}, f32[1,1,256]{2,1,0:T(1,128)S(1)}, u32[]{:S(2)}) copy-start(f32[1,1,256]{2,1,0:T(1,128)S(1)} %get-tuple-element.80) | copy-start | bytes 3076
  14.9 13.5 %copy-start.17 = (f32[1,1,256]{2,1,0:T(1,128)}, f32[1,1,256]{2,1,0:T(1,128)S(1)}, u32[]{:S(2)}) copy-start(f32[1,1,256]{2,1,0:T(1,128)S(1)} %get-tuple-element.81) | copy-start | bytes 3076
  14.9 13.5 %copy-start.19 = (f32[1,1,256]{2,1,0:T(1,128)}, f32[1,1,256]{2,1,0:T(1,128)S(1)}, u32[]{:S(2)}) copy-start(f32[1,1,256]{2,1,0:T(1,128)S(1)} %get-tuple-element.82) | copy-start | bytes 3076
  14.9 13.5 %copy-start.21 = (f32[1,1,256]{2,1,0:T(1,128)}, f32[1,1,256]{2,1,0:T(1,128)S(1)}, u32[]{:S(2)}) copy-start(f32[1,1,256]{2,1,0:T(1,128)S(1)} %get-tuple-element.83) | copy-start | bytes 3076
  14.9 13.5 %copy-start.23 = (f32[1,1,256]{2,1,0:T(1,128)}, f32[1,1,256]{2,1,0:T(1,128)S(1)}, u32[]{:S(2)}) copy-start(f32[1,1,256]{2,1,0:T(1,128)S(1)} %get-tuple-element.84) | copy-start | bytes 3076
  14.9 13.5 %copy-start.25 = (f32[1,1,256]{2,1,0:T(1,128)}, f32[1,1,256]{2,1,0:T(1,128)S(1)}, u32[]{:S(2)}) copy-start(f32[1,1,256]{2,1,0:T(1,128)S(1)} %get-tuple-element.85) | copy-start | bytes 3076
  15.0 13.5 %copy-start.27 = (f32[1,1,256]{2,1,0:T(1,128)}, f32[1,1,256]{2,1,0:T(1,128)S(1)}, u32[]{:S(2)}) copy-start(f32[1,1,256]{2,1,0:T(1,128)S(1)} %get-tuple-element.86) | copy-start | bytes 3076
  15.0 13.5 %copy-start.29 = (f32[1,1,256]{2,1,0:T(1,128)}, f32[1,1,256]{2,1,0:T(1,128)S(1)}, u32[]{:S(2)}) copy-start(f32[1,1,256]{2,1,0:T(1,128)S(1)} %get-tuple-element.87) | copy-start | bytes 3076
  15.0 13.5 %copy-start.31 = (f32[1,1,256]{2,1,0:T(1,128)}, f32[1,1,256]{2,1,0:T(1,128)S(1)}, u32[]{:S(2)}) copy-start(f32[1,1,256]{2,1,0:T(1,128)S(1)} %get-tuple-element.88) | copy-start | bytes 3076
  15.0 13.5 %copy-start.33 = (f32[1,1,256]{2,1,0:T(1,128)}, f32[1,1,256]{2,1,0:T(1,128)S(1)}, u32[]{:S(2)}) copy-start(f32[1,1,256]{2,1,0:T(1,128)S(1)} %get-tuple-element.89) | copy-start | bytes 3076
  15.0 13.5 %copy-start.35 = (f32[1,1,256]{2,1,0:T(1,128)}, f32[1,1,256]{2,1,0:T(1,128)S(1)}, u32[]{:S(2)}) copy-start(f32[1,1,256]{2,1,0:T(1,128)S(1)} %get-tuple-element.90) | copy-start | bytes 3076
  15.0 13.5 %copy-start.37 = (f32[1,1,256]{2,1,0:T(1,128)}, f32[1,1,256]{2,1,0:T(1,128)S(1)}, u32[]{:S(2)}) copy-start(f32[1,1,256]{2,1,0:T(1,128)S(1)} %get-tuple-element.91) | copy-start | bytes 3076
  18.6 8.4 %collective-permute-start.2 = (bf16[1,3,22,256]{3,2,1,0:T(8,128)(2,1)S(1)}, bf16[1,3,22,256]{3,2,1,0:T(8,128)(2,1)S(1)}, u32[]{:S(2)}, u32[]{:S(2)}) collective-permute-start(bf16[1,3,22,256]{3,2,1,0:T(8,128)(2,1)S(1)} %get-tuple-element.74), channel_id=1, source_target_pairs={{0,1},{2,3},{4,5},{6,7},{8,9},{10,11},{12,13},{14,15},{16,17},{18,... | collective-permute-start | bytes 101384 | tf_op jit(solution)/shard_map/ppermute | solution.py:20
  22.4 5.9 %collective-permute-start.3 = (bf16[1,3,22,256]{3,2,1,0:T(8,128)(2,1)S(1)}, bf16[1,3,22,256]{3,2,1,0:T(8,128)(2,1)S(1)}, u32[]{:S(2)}, u32[]{:S(2)}) collective-permute-start(bf16[1,3,22,256]{3,2,1,0:T(8,128)(2,1)S(1)} %get-tuple-element.75), channel_id=1, source_target_pairs={{1,0},{3,2},{5,4},{7,6},{9,8},{11,10},{13,12},{15,14},{17,16},{19,... | collective-permute-start | bytes 101384 | tf_op jit(solution)/shard_map/ppermute | solution.py:22
  57.9 57.9 %copy-start.7 = (f32[1,32,16,256]{3,2,1,0:T(8,128)S(1)}, f32[1,32,16,256]{3,2,1,0:T(8,128)}, u32[]{:S(2)}) copy-start(f32[1,32,16,256]{3,2,1,0:T(8,128)} %reshape.366) | copy-start | bytes 1572868
  57.9 57.9 %copy-start.16 = (f32[1,1,256]{2,1,0:T(1,128)S(1)}, f32[1,1,256]{2,1,0:T(1,128)}, u32[]{:S(2)}) copy-start(f32[1,1,256]{2,1,0:T(1,128)} %copy-done.15) | copy-start | bytes 3076
  57.9 57.9 %copy-start.18 = (f32[1,1,256]{2,1,0:T(1,128)S(1)}, f32[1,1,256]{2,1,0:T(1,128)}, u32[]{:S(2)}) copy-start(f32[1,1,256]{2,1,0:T(1,128)} %copy-done.17) | copy-start | bytes 3076
  57.9 57.9 %copy-start.20 = (f32[1,1,256]{2,1,0:T(1,128)S(1)}, f32[1,1,256]{2,1,0:T(1,128)}, u32[]{:S(2)}) copy-start(f32[1,1,256]{2,1,0:T(1,128)} %copy-done.19) | copy-start | bytes 3076
  58.0 57.9 %copy-start.22 = (f32[1,1,256]{2,1,0:T(1,128)S(1)}, f32[1,1,256]{2,1,0:T(1,128)}, u32[]{:S(2)}) copy-start(f32[1,1,256]{2,1,0:T(1,128)} %copy-done.21) | copy-start | bytes 3076
  58.0 57.9 %copy-start.24 = (f32[1,1,256]{2,1,0:T(1,128)S(1)}, f32[1,1,256]{2,1,0:T(1,128)}, u32[]{:S(2)}) copy-start(f32[1,1,256]{2,1,0:T(1,128)} %copy-done.23) | copy-start | bytes 3076
  58.0 57.9 %copy-start.26 = (f32[1,1,256]{2,1,0:T(1,128)S(1)}, f32[1,1,256]{2,1,0:T(1,128)}, u32[]{:S(2)}) copy-start(f32[1,1,256]{2,1,0:T(1,128)} %copy-done.25) | copy-start | bytes 3076
  58.0 57.9 %copy-start.28 = (f32[1,1,256]{2,1,0:T(1,128)S(1)}, f32[1,1,256]{2,1,0:T(1,128)}, u32[]{:S(2)}) copy-start(f32[1,1,256]{2,1,0:T(1,128)} %copy-done.27) | copy-start | bytes 3076
  58.0 57.9 %copy-start.30 = (f32[1,1,256]{2,1,0:T(1,128)S(1)}, f32[1,1,256]{2,1,0:T(1,128)}, u32[]{:S(2)}) copy-start(f32[1,1,256]{2,1,0:T(1,128)} %copy-done.29) | copy-start | bytes 3076
  58.0 57.9 %copy-start.32 = (f32[1,1,256]{2,1,0:T(1,128)S(1)}, f32[1,1,256]{2,1,0:T(1,128)}, u32[]{:S(2)}) copy-start(f32[1,1,256]{2,1,0:T(1,128)} %copy-done.31) | copy-start | bytes 3076
  58.0 57.9 %copy-start.34 = (f32[1,1,256]{2,1,0:T(1,128)S(1)}, f32[1,1,256]{2,1,0:T(1,128)}, u32[]{:S(2)}) copy-start(f32[1,1,256]{2,1,0:T(1,128)} %copy-done.33) | copy-start | bytes 3076
  58.0 57.9 %copy-start.36 = (f32[1,1,256]{2,1,0:T(1,128)S(1)}, f32[1,1,256]{2,1,0:T(1,128)}, u32[]{:S(2)}) copy-start(f32[1,1,256]{2,1,0:T(1,128)} %copy-done.35) | copy-start | bytes 3076
  58.0 57.9 %copy-start.38 = (f32[1,1,256]{2,1,0:T(1,128)S(1)}, f32[1,1,256]{2,1,0:T(1,128)}, u32[]{:S(2)}) copy-start(f32[1,1,256]{2,1,0:T(1,128)} %copy-done.37) | copy-start | bytes 3076
  58.0 57.9 %copy-start.40 = (f32[1,1,256]{2,1,0:T(1,128)S(1)}, f32[1,1,256]{2,1,0:T(1,128)}, u32[]{:S(2)}) copy-start(f32[1,1,256]{2,1,0:T(1,128)} %copy-done.39) | copy-start | bytes 3076
  58.1 57.9 %copy-start.42 = (f32[1,1,256]{2,1,0:T(1,128)S(1)}, f32[1,1,256]{2,1,0:T(1,128)}, u32[]{:S(2)}) copy-start(f32[1,1,256]{2,1,0:T(1,128)} %copy-done.41) | copy-start | bytes 3076
  58.1 57.9 %copy-start.44 = (f32[1,1,256]{2,1,0:T(1,128)S(1)}, f32[1,1,256]{2,1,0:T(1,128)}, u32[]{:S(2)}) copy-start(f32[1,1,256]{2,1,0:T(1,128)} %copy-done.43) | copy-start | bytes 3076
  58.1 57.9 %copy-start.46 = (f32[1,1,256]{2,1,0:T(1,128)S(1)}, f32[1,1,256]{2,1,0:T(1,128)}, u32[]{:S(2)}) copy-start(f32[1,1,256]{2,1,0:T(1,128)} %copy-done.45) | copy-start | bytes 3076
  58.1 57.9 %copy-start.48 = (f32[1,1,256]{2,1,0:T(1,128)S(1)}, f32[1,1,256]{2,1,0:T(1,128)}, u32[]{:S(2)}) copy-start(f32[1,1,256]{2,1,0:T(1,128)} %copy-done.47) | copy-start | bytes 3076
  58.1 57.9 %copy-start.50 = (f32[1,1,256]{2,1,0:T(1,128)S(1)}, f32[1,1,256]{2,1,0:T(1,128)}, u32[]{:S(2)}) copy-start(f32[1,1,256]{2,1,0:T(1,128)} %copy-done.49) | copy-start | bytes 3076
  58.1 57.9 %copy-start.52 = (f32[1,1,256]{2,1,0:T(1,128)S(1)}, f32[1,1,256]{2,1,0:T(1,128)}, u32[]{:S(2)}) copy-start(f32[1,1,256]{2,1,0:T(1,128)} %copy-done.51) | copy-start | bytes 3076
  58.1 57.9 %copy-start.54 = (f32[1,1,256]{2,1,0:T(1,128)S(1)}, f32[1,1,256]{2,1,0:T(1,128)}, u32[]{:S(2)}) copy-start(f32[1,1,256]{2,1,0:T(1,128)} %copy-done.53) | copy-start | bytes 3076
  58.1 57.9 %copy-start.56 = (f32[1,1,256]{2,1,0:T(1,128)S(1)}, f32[1,1,256]{2,1,0:T(1,128)}, u32[]{:S(2)}) copy-start(f32[1,1,256]{2,1,0:T(1,128)} %copy-done.55) | copy-start | bytes 3076
  58.1 57.9 %copy-start.58 = (f32[1,1,256]{2,1,0:T(1,128)S(1)}, f32[1,1,256]{2,1,0:T(1,128)}, u32[]{:S(2)}) copy-start(f32[1,1,256]{2,1,0:T(1,128)} %copy-done.57) | copy-start | bytes 3076
  58.1 57.9 %copy-start.60 = (f32[1,1,256]{2,1,0:T(1,128)S(1)}, f32[1,1,256]{2,1,0:T(1,128)}, u32[]{:S(2)}) copy-start(f32[1,1,256]{2,1,0:T(1,128)} %copy-done.59) | copy-start | bytes 3076
  58.2 57.9 %copy-start.62 = (f32[1,1,256]{2,1,0:T(1,128)S(1)}, f32[1,1,256]{2,1,0:T(1,128)}, u32[]{:S(2)}) copy-start(f32[1,1,256]{2,1,0:T(1,128)} %copy-done.61) | copy-start | bytes 3076
  58.2 57.9 %copy-start.64 = (f32[1,1,256]{2,1,0:T(1,128)S(1)}, f32[1,1,256]{2,1,0:T(1,128)}, u32[]{:S(2)}) copy-start(f32[1,1,256]{2,1,0:T(1,128)} %copy-done.63) | copy-start | bytes 3076
  58.2 57.9 %copy-start.66 = (f32[1,1,256]{2,1,0:T(1,128)S(1)}, f32[1,1,256]{2,1,0:T(1,128)}, u32[]{:S(2)}) copy-start(f32[1,1,256]{2,1,0:T(1,128)} %copy-done.65) | copy-start | bytes 3076
  58.2 57.9 %copy-start.68 = (f32[1,1,256]{2,1,0:T(1,128)S(1)}, f32[1,1,256]{2,1,0:T(1,128)}, u32[]{:S(2)}) copy-start(f32[1,1,256]{2,1,0:T(1,128)} %copy-done.67) | copy-start | bytes 3076
  58.2 57.9 %copy-start.70 = (f32[1,1,256]{2,1,0:T(1,128)S(1)}, f32[1,1,256]{2,1,0:T(1,128)}, u32[]{:S(2)}) copy-start(f32[1,1,256]{2,1,0:T(1,128)} %copy-done.69) | copy-start | bytes 3076
  58.2 57.9 %copy-start.72 = (f32[1,1,256]{2,1,0:T(1,128)S(1)}, f32[1,1,256]{2,1,0:T(1,128)}, u32[]{:S(2)}) copy-start(f32[1,1,256]{2,1,0:T(1,128)} %copy-done.71) | copy-start | bytes 3076
  58.2 57.9 %copy-start.74 = (f32[1,1,256]{2,1,0:T(1,128)S(1)}, f32[1,1,256]{2,1,0:T(1,128)}, u32[]{:S(2)}) copy-start(f32[1,1,256]{2,1,0:T(1,128)} %copy-done.73) | copy-start | bytes 3076
  58.2 57.9 %copy-start.76 = (f32[1,1,256]{2,1,0:T(1,128)S(1)}, f32[1,1,256]{2,1,0:T(1,128)}, u32[]{:S(2)}) copy-start(f32[1,1,256]{2,1,0:T(1,128)} %copy-done.75) | copy-start | bytes 3076
  58.2 57.9 %copy-start.78 = (f32[1,1,256]{2,1,0:T(1,128)S(1)}, f32[1,1,256]{2,1,0:T(1,128)}, u32[]{:S(2)}) copy-start(f32[1,1,256]{2,1,0:T(1,128)} %copy-done.77) | copy-start | bytes 3076
  58.2 57.9 %copy-start.80 = (f32[1,1,256]{2,1,0:T(1,128)S(1)}, f32[1,1,256]{2,1,0:T(1,128)}, u32[]{:S(2)}) copy-start(f32[1,1,256]{2,1,0:T(1,128)} %copy-done.79) | copy-start | bytes 3076
  58.3 57.9 %copy-start.82 = (f32[1,1,256]{2,1,0:T(1,128)S(1)}, f32[1,1,256]{2,1,0:T(1,128)}, u32[]{:S(2)}) copy-start(f32[1,1,256]{2,1,0:T(1,128)} %copy-done.81) | copy-start | bytes 3076
  58.3 57.9 %copy-start.84 = (f32[1,1,256]{2,1,0:T(1,128)S(1)}, f32[1,1,256]{2,1,0:T(1,128)}, u32[]{:S(2)}) copy-start(f32[1,1,256]{2,1,0:T(1,128)} %copy-done.83) | copy-start | bytes 3076
  58.3 57.9 %copy-start.86 = (f32[1,1,256]{2,1,0:T(1,128)S(1)}, f32[1,1,256]{2,1,0:T(1,128)}, u32[]{:S(2)}) copy-start(f32[1,1,256]{2,1,0:T(1,128)} %copy-done.85) | copy-start | bytes 3076
  58.3 57.9 %copy-start.88 = (f32[1,1,256]{2,1,0:T(1,128)S(1)}, f32[1,1,256]{2,1,0:T(1,128)}, u32[]{:S(2)}) copy-start(f32[1,1,256]{2,1,0:T(1,128)} %copy-done.87) | copy-start | bytes 3076
  58.3 57.9 %copy-start.90 = (f32[1,1,256]{2,1,0:T(1,128)S(1)}, f32[1,1,256]{2,1,0:T(1,128)}, u32[]{:S(2)}) copy-start(f32[1,1,256]{2,1,0:T(1,128)} %copy-done.89) | copy-start | bytes 3076
  58.3 57.9 %copy-start.92 = (f32[1,1,256]{2,1,0:T(1,128)S(1)}, f32[1,1,256]{2,1,0:T(1,128)}, u32[]{:S(2)}) copy-start(f32[1,1,256]{2,1,0:T(1,128)} %copy-done.91) | copy-start | bytes 3076
  61.3 44.3 %collective-permute-start.4 = (bf16[1,32,3,256]{3,2,1,0:T(4,128)(2,1)S(1)}, bf16[1,32,3,256]{3,2,1,0:T(4,128)(2,1)S(1)}, u32[]{:S(2)}, u32[]{:S(2)}) collective-permute-start(bf16[1,32,3,256]{3,2,1,0:T(4,128)(2,1)S(1)} %get-tuple-element.76), channel_id=1, source_target_pairs={{0,2},{2,4},{4,6},{6,8},{8,10},{10,12},{12,14},{14,16},{16,18},{18... | collective-permute-start | bytes 147464 | tf_op jit(solution)/shard_map/ppermute | solution.py:20
  61.4 44.2 %collective-permute-start.5 = (bf16[1,32,3,256]{3,2,1,0:T(4,128)(2,1)S(1)}, bf16[1,32,3,256]{3,2,1,0:T(4,128)(2,1)S(1)}, u32[]{:S(2)}, u32[]{:S(2)}) collective-permute-start(bf16[1,32,3,256]{3,2,1,0:T(4,128)(2,1)S(1)} %get-tuple-element.77), channel_id=1, source_target_pairs={{2,0},{4,2},{6,4},{8,6},{10,8},{12,10},{14,12},{16,14},{18,16},{20... | collective-permute-start | bytes 147464 | tf_op jit(solution)/shard_map/ppermute | solution.py:22
  103.9 17.3 %copy-start.12 = (f32[7,7,256]{2,1,0:T(8,128)}, f32[7,7,256]{2,1,0:T(8,128)S(1)}, u32[]{:S(2)}) copy-start(f32[7,7,256]{2,1,0:T(8,128)S(1)} %get-tuple-element.59) | copy-start | bytes 150532
  104.0 17.3 %copy-start.94 = (f32[256]{0:T(256)}, f32[256]{0:T(256)S(1)}, u32[]{:S(2)}) copy-start(f32[256]{0:T(256)S(1)} %get-tuple-element.60) | copy-start | bytes 3076
  104.0 17.3 %copy-start.96 = (f32[256]{0:T(256)}, f32[256]{0:T(256)S(1)}, u32[]{:S(2)}) copy-start(f32[256]{0:T(256)S(1)} %get-tuple-element.61) | copy-start | bytes 3076
  105.6 7.4 %collective-permute-start.6 = (bf16[1,3,22,256]{3,2,1,0:T(8,128)(2,1)S(1)}, bf16[1,3,22,256]{3,2,1,0:T(8,128)(2,1)S(1)}, u32[]{:S(2)}, u32[]{:S(2)}) collective-permute-start(bf16[1,3,22,256]{3,2,1,0:T(8,128)(2,1)S(1)} %get-tuple-element.72), channel_id=1, source_target_pairs={{0,1},{2,3},{4,5},{6,7},{8,9},{10,11},{12,13},{14,15},{16,17},{18,... | collective-permute-start | bytes 101384 | tf_op jit(solution)/shard_map/ppermute | solution.py:20
  109.8 5.9 %collective-permute-start.7 = (bf16[1,3,22,256]{3,2,1,0:T(8,128)(2,1)S(1)}, bf16[1,3,22,256]{3,2,1,0:T(8,128)(2,1)S(1)}, u32[]{:S(2)}, u32[]{:S(2)}) collective-permute-start(bf16[1,3,22,256]{3,2,1,0:T(8,128)(2,1)S(1)} %get-tuple-element.73), channel_id=1, source_target_pairs={{1,0},{3,2},{5,4},{7,6},{9,8},{11,10},{13,12},{15,14},{17,16},{19,... | collective-permute-start | bytes 101384 | tf_op jit(solution)/shard_map/ppermute | solution.py:22
  (44 other events, 379.4 us)
Sparse Core Ops, SparseCore 0:
  57.3 143.0 all-reduce.3
where the time goes:
time: 221 us
  waiting for transfers between devices  83.1 us (38%)
  blocking collectives  38.1 us (17%)
  other arithmetic  29.6 us (13%)
  starting transfers between devices  20.6 us (9%)
  between operations  19.6 us (9%)
  matrix products  16.1 us (7%)
  local copies, waits for them, and re-layouts  13.5 us (6%)
    psum x1, waiting for transfers between devices, body(): lax.psum((raw_kernel, unclipped_gain, raw_inner, raw_outer, raw_scale), (...  79.2 us
    psum x1, blocking collectives, body(): lax.psum((raw_kernel, unclipped_gain, raw_inner, raw_outer, raw_scale), (...  38.1 us
    ppermute x4, starting transfers between devices, padded_2(): lax.ppermute(head, axis, [((i + 1) % count, i) for i in range(ends)])  12.1 us
    ppermute x4, starting transfers between devices, padded_2(): lax.ppermute(tail, axis, [(i, (i + 1) % count) for i in range(ends)])  8.5 us
    dot_general x1, matrix products, body(): jnp.dot(normalized_output, inner_weight, preferred_element_type=jnp.float32)  5.79 us
    convert_element_type x1, other arithmetic, body(): (grad_blocked.reshape(field.shape).astype(jnp.float32) + spread).astype(j...  5.07 us
    reduce_sum x3, other arithmetic, kernel_terms(): jnp.sum(padded[:, row_shift:row_shift + rows, col_shift:col_shift + cols]...  4.77 us
    reduce_sum x1, other arithmetic, body(): centered_input = mixed - jnp.mean(mixed, axis=-1, keepdims=True)  4.53 us
  transfers between devices with their start and end apart: 9, of which 3 were waited for; matrix products, arithmetic and copies ran while one was open for 8% of the time, Pallas kernels for 0%

commit v1 on v0

--- a/solution.py
+++ b/solution.py
@@ -160,7 +160,7 @@
     summed_down = reduce_down(raw_down)
     limit = math.sqrt(PARAMS)
     sum_kernel, sum_gain, sum_inner, sum_outer, sum_scale = lax.psum(
-        (raw_kernel, unclipped_gain, raw_inner, raw_outer, raw_scale), ("lon", "lat")
+        lax.psum((raw_kernel, unclipped_gain, raw_inner, raw_outer, raw_scale), "lat"), "lon"
     )
     total = (
         jnp.sum(sum_kernel * sum_kernel)

time: 221 us -> 369 us (1.67)
  waiting for transfers between devices: 83.1 us -> 203 us
  blocking collectives: 38.1 us -> 67.9 us
    psum x1 -> x3, waiting for transfers between devices: 79.2 us -> 199 us  [the longest x1 101 us: reduce_down(): return lax.psum(raw_down, ('lon', 'lat'))]
    psum x1 -> x2, blocking collectives: 38.1 us -> 67.9 us  [the longest x1 57.8 us: body(): lax.psum(lax.psum((raw_kernel, unclipped_gain, raw_inner, raw_outer, raw_...]
  transfers between devices with their start and end apart: 9 -> 11, of which waited for: 3 -> 4; matrix products, arithmetic and copies ran while one was open for 8% -> 8% of each run, Pallas kernels for 0% -> 0%
where the time goes in v1:
time: 369 us; the launch traced here: 368 us
  waiting for transfers between devices  203 us (55%)
  blocking collectives  67.9 us (18%)
  other arithmetic  32 us (9%)
  between operations  19.5 us (5%)
  starting transfers between devices  19.4 us (5%)
  matrix products  15.5 us (4%)
  local copies, waits for them, and re-layouts  11 us (3%)
    psum x1, waiting for transfers between devices, reduce_down(): return lax.psum(raw_down, ('lon', 'lat'))  101 us
    psum x1, waiting for transfers between devices, body(): lax.psum(lax.psum((raw_kernel, unclipped_gain, raw_inner, raw_outer, raw_...  97.9 us
    psum x1, blocking collectives, body(): lax.psum(lax.psum((raw_kernel, unclipped_gain, raw_inner, raw_outer, raw_...  57.8 us
    ppermute x4, starting transfers between devices, padded_2(): lax.ppermute(head, axis, [((i + 1) % count, i) for i in range(ends)])  12.1 us
    psum x1, blocking collectives, body(): lax.psum((raw_kernel, unclipped_gain, raw_inner, raw_outer, raw_scale), '...  10 us
  transfers between devices with their start and end apart: 11, of which 4 were waited for; matrix products, arithmetic and copies ran while one was open for 8% of the time, Pallas kernels for 0%

profile of v1, /device:TPU:0, one launch (start us, length us, event | category | flops | bytes accessed | tf_op | source)
XLA Modules:
  0.0 368.4 jit_solution(1904691904731222047)
XLA Ops:
  7.2 0.0 all-reduce.12.cloned.1.call-start
  7.2 1.1 fusion.114
  8.3 0.5 collective-permute-start
  8.8 5.1 %collective-permute-start.1 = (bf16[1,32,3,256]{3,2,1,0:T(4,128)(2,1)S(1)}, bf16[1,32,3,256]{3,2,1,0:T(4,128)(2,1)S(1)}, u32[]{:S(2)}, u32[]{:S(2)}) collective-permute-start(bf16[1,32,3,256]{3,2,1,0:T(4,128)(2,1)S(1)} %get-tuple-element.83), channel_id=1, source_target_pairs={{2,0},{4,2},{6,4},{8,6},{10,8},{12,10},{14,12},{16,14},{18,16},{20... | collective-permute-start | bytes 147464 | tf_op jit(solution)/shard_map/ppermute | solution.py:22
  13.9 1.0 fusion.115
  15.1 1.4 convolution_convert_fusion
  16.5 1.0 fusion.116
  17.8 0.8 pad_maximum_fusion.5
  18.6 3.8 %collective-permute-start.2 = (bf16[1,3,22,256]{3,2,1,0:T(8,128)(2,1)S(1)}, bf16[1,3,22,256]{3,2,1,0:T(8,128)(2,1)S(1)}, u32[]{:S(2)}, u32[]{:S(2)}) collective-permute-start(bf16[1,3,22,256]{3,2,1,0:T(8,128)(2,1)S(1)} %get-tuple-element.78), channel_id=1, source_target_pairs={{0,1},{2,3},{4,5},{6,7},{8,9},{10,11},{12,13},{14,15},{16,17},{18,... | collective-permute-start | bytes 101384 | tf_op jit(solution)/shard_map/ppermute | solution.py:20
  22.4 1.3 collective-permute-start.3
  23.7 1.5 fusion.117
  25.2 0.2 copy.21
  25.4 0.4 reshape.367
  25.8 1.2 reshape.366
  26.9 1.3 collective-permute-done.3
  28.2 0.2 maximum_convert_fusion
  28.8 4.5 %fusion.112 = (f32[32,16]{1,0:T(8,128)S(1)}, f32[1,32,16,256]{3,2,1,0:T(8,128)S(1)}) fusion(f32[1,38,22,256]{3,2,1,0:T(8,128)S(1)} %maximum_convert_fusion, f32[256]{0:T(256)} %bitcast.49, f32[256]{0:T(256)} %bitcast.48, f32[256]{0:T(256)S(1)} %bitcast.144, f32[256]{0:T(256)S(1)} %bitcast.146, f32[256]{0:T(256)S(1)} %bitcast.148, f32[256]{0:T(256)S(1)} %bitcast.150, ...), kind=kLoop, calls=%fused_computation.259 | loop fusion | flops 12844544 | bytes 26266624 | tf_op jit(solution)/shard_map/reduce_sum | solution.py:110
  33.4 0.2 multiply_reduce_fusion.7
  33.7 0.2 multiply_convert_fusion.3
  33.9 0.1 copy-done.8
  34.0 0.3 copy-done.9
  34.3 5.8 %multiply_convert_fusion = (bf16[512,1024]{1,0:T(8,128)(2,1)S(1)}, f32[512,1024]{1,0:T(8,128)S(1)}, f32[512,1024]{1,0:T(8,128)S(1)}) fusion(bf16[512,256]{1,0:T(8,128)(2,1)S(1)} %bitcast.138, bf16[256,1024]{1,0:T(8,128)(2,1)S(1)} %copy-done.114), kind=kOutput, calls=%fused_computation.53 | convolution fusion | flops 302514176 | bytes 6029312 | tf_op jit(solution)/shard_map/dot_general | solution.py:118
  40.1 1.5 fusion.110
  41.6 1.0 multiply_reduce_fusion.3
  42.6 1.0 add_convert_fusion
  43.6 0.6 multiply_reduce_fusion.6
  44.2 1.4 fusion.118
  45.7 0.2 all-reduce.8.cloned.1.call-start
  45.9 0.6 broadcast_multiply_fusion.6
  46.5 0.1 reshape_reshape.4
  46.6 0.9 copy.22
  47.5 1.1 reshape.359
  48.6 1.4 div.20
  50.0 1.6 multiply_reduce_fusion.4
  51.6 3.0 fusion.54
  54.6 0.7 fusion.53
  55.5 1.1 fusion.55
  56.7 0.2 stack.199
  56.9 1.8 fusion.107
  58.7 0.0 all-reduce.10.cloned.1.call-start
  58.8 0.1 fusion.113
  58.8 0.1 collective-permute-start.4
  58.9 4.4 %collective-permute-start.5 = (bf16[1,32,3,256]{3,2,1,0:T(4,128)(2,1)S(1)}, bf16[1,32,3,256]{3,2,1,0:T(4,128)(2,1)S(1)}, u32[]{:S(2)}, u32[]{:S(2)}) collective-permute-start(bf16[1,32,3,256]{3,2,1,0:T(4,128)(2,1)S(1)} %get-tuple-element.81), channel_id=1, source_target_pairs={{2,0},{4,2},{6,4},{8,6},{10,8},{12,10},{14,12},{16,14},{18,16},{20... | collective-permute-start | bytes 147464 | tf_op jit(solution)/shard_map/ppermute | solution.py:22
  63.3 10.0 %all-reduce.2 = (f32[7,7,256]{2,1,0:T(8,128)S(1)}, f32[256]{0:T(256)S(1)}, f32[256]{0:T(256)S(1)}) all-reduce(f32[7,7,256]{2,1,0:T(8,128)S(1)} %reshape.363, f32[256]{0:T(256)S(1)} %copy-done.109, f32[256]{0:T(256)S(1)} %copy-done.108), channel_id=1, replica_groups=mesh['lon'=16,'lat'=2] {'lat'}, use_global_device_ids=true, to_apply=%region_53.0 | all-reduce | flops 13056 | bytes 104448 | tf_op jit(solution)/shard_map/psum | solution.py:163
  73.4 57.8 %all-reduce = (f32[7,7,256]{2,1,0:T(8,128)S(1)}, f32[256]{0:T(256)S(1)}, f32[256]{0:T(256)S(1)}) all-reduce(f32[7,7,256]{2,1,0:T(8,128)S(1)} %get-tuple-element.64, f32[256]{0:T(256)S(1)} %get-tuple-element.65, f32[256]{0:T(256)S(1)} %get-tuple-element.66), channel_id=1, replica_groups=mesh['lon'=16,'lat'=2] {'lon'}, use_global_device_ids=true, to_apply=%region_54.0 | all-reduce | flops 13056 | bytes 104448 | tf_op jit(solution)/shard_map/psum | solution.py:162
  131.2 0.6 multiply_reduce_fusion.8
  131.8 1.0 fusion.6
  133.2 0.7 multiply_reduce_fusion.9
  133.9 2.7 collective-permute-start.6
  136.6 1.3 collective-permute-start.7
  137.9 0.6 multiply_reduce_fusion.10
  139.8 2.6 collective-permute-done.7
  142.5 0.2 maximum_convert_fusion.1
  143.1 5.1 %fusion.58 = bf16[1,32,16,256]{3,2,1,0:T(8,128)(2,1)} fusion(f32[1,32,16,256]{3,2,1,0:T(8,128)S(1)} %copy-done.5, f32[1,38,22,256]{3,2,1,0:T(8,128)S(1)} %maximum_convert_fusion.1, f32[256]{0:T(256)} %bitcast.49, f32[256]{0:T(256)} %bitcast.48, f32[256]{0:T(256)S(1)} %bitcast.145, f32[256]{0:T(256)S(1)} %bitcast.147, f32[256]{0:T(256)S(1)} %bitcast.149, ...), kind=kLoop, calls=%fused_computation.125 | loop fusion | flops 12976128 | bytes 26526720 | tf_op jit(solution)/shard_map/convert_element_type | solution.py:156
  148.2 101.3 %all-reduce.8.cloned.1.call-done = f32[1024,512]{1,0:T(8,128)} async-done(((f32[1024,512]{1,0:T(8,128)}), f32[1024,512]{1,0:T(8,128)}) %all-reduce.8.cloned.1.call-update) | async-done | bytes 2097168 | tf_op jit(solution)/shard_map/psum | solution.py:93
  249.5 2.7 multiply_reduce_fusion
  252.2 97.9 %all-reduce.10.cloned.1.call-done = (f32[256,1024]{1,0:T(8,128)}, f32[1024,256]{1,0:T(8,128)}) async-done(((f32[256,1024]{1,0:T(8,128)}, f32[1024,256]{1,0:T(8,128)}), (f32[256,1024]{1,0:T(8,128)}, f32[1024,256]{1,0:T(8,128)})) %all-reduce.10.cloned.1.call-update) | async-done | bytes 2097168 | tf_op jit(solution)/shard_map/psum | solution.py:162
  350.1 2.2 multiply_reduce_fusion.1
  352.3 2.1 multiply_reduce_fusion.2
  357.1 1.0 broadcast_multiply_fusion.1
  358.1 1.0 broadcast_multiply_fusion.2
  359.2 0.6 broadcast_multiply_fusion.3
  359.8 0.6 broadcast_multiply_fusion.7
  360.4 1.5 broadcast_multiply_fusion
  (243 shorter events, 0.7 us)
Async XLA Ops:
  7.2 135.5 %all-reduce.12.cloned.1.call-start = ((), (), s32[]{:S(2)}) async-start(), calls=%async_computation.2 | async-start | bytes 4194304 | tf_op jit(solution)/shard_map/psum | solution.py:163
  8.3 9.4 %collective-permute-start = (bf16[1,32,3,256]{3,2,1,0:T(4,128)(2,1)S(1)}, bf16[1,32,3,256]{3,2,1,0:T(4,128)(2,1)S(1)}, u32[]{:S(2)}, u32[]{:S(2)}) collective-permute-start(bf16[1,32,3,256]{3,2,1,0:T(4,128)(2,1)S(1)} %get-tuple-element.82), channel_id=1, source_target_pairs={{0,2},{2,4},{4,6},{6,8},{8,10},{10,12},{12,14},{14,16},{16,18},{18... | collective-permute-start | bytes 147464 | tf_op jit(solution)/shard_map/ppermute | solution.py:20
  8.8 8.9 %collective-permute-start.1 = (bf16[1,32,3,256]{3,2,1,0:T(4,128)(2,1)S(1)}, bf16[1,32,3,256]{3,2,1,0:T(4,128)(2,1)S(1)}, u32[]{:S(2)}, u32[]{:S(2)}) collective-permute-start(bf16[1,32,3,256]{3,2,1,0:T(4,128)(2,1)S(1)} %get-tuple-element.83), channel_id=1, source_target_pairs={{2,0},{4,2},{6,4},{8,6},{10,8},{12,10},{14,12},{16,14},{18,16},{20... | collective-permute-start | bytes 147464 | tf_op jit(solution)/shard_map/ppermute | solution.py:22
  14.9 13.5 %copy-start.11 = (f32[1,1,256]{2,1,0:T(1,128)}, f32[1,1,256]{2,1,0:T(1,128)S(1)}, u32[]{:S(2)}) copy-start(f32[1,1,256]{2,1,0:T(1,128)S(1)} %get-tuple-element.84) | copy-start | bytes 3076
  14.9 13.5 %copy-start.13 = (f32[1,1,256]{2,1,0:T(1,128)}, f32[1,1,256]{2,1,0:T(1,128)S(1)}, u32[]{:S(2)}) copy-start(f32[1,1,256]{2,1,0:T(1,128)S(1)} %get-tuple-element.85) | copy-start | bytes 3076
  14.9 13.5 %copy-start.15 = (f32[1,1,256]{2,1,0:T(1,128)}, f32[1,1,256]{2,1,0:T(1,128)S(1)}, u32[]{:S(2)}) copy-start(f32[1,1,256]{2,1,0:T(1,128)S(1)} %get-tuple-element.86) | copy-start | bytes 3076
  14.9 13.5 %copy-start.17 = (f32[1,1,256]{2,1,0:T(1,128)}, f32[1,1,256]{2,1,0:T(1,128)S(1)}, u32[]{:S(2)}) copy-start(f32[1,1,256]{2,1,0:T(1,128)S(1)} %get-tuple-element.87) | copy-start | bytes 3076
  14.9 13.5 %copy-start.19 = (f32[1,1,256]{2,1,0:T(1,128)}, f32[1,1,256]{2,1,0:T(1,128)S(1)}, u32[]{:S(2)}) copy-start(f32[1,1,256]{2,1,0:T(1,128)S(1)} %get-tuple-element.88) | copy-start | bytes 3076
  14.9 13.5 %copy-start.21 = (f32[1,1,256]{2,1,0:T(1,128)}, f32[1,1,256]{2,1,0:T(1,128)S(1)}, u32[]{:S(2)}) copy-start(f32[1,1,256]{2,1,0:T(1,128)S(1)} %get-tuple-element.89) | copy-start | bytes 3076
  15.0 13.5 %copy-start.23 = (f32[1,1,256]{2,1,0:T(1,128)}, f32[1,1,256]{2,1,0:T(1,128)S(1)}, u32[]{:S(2)}) copy-start(f32[1,1,256]{2,1,0:T(1,128)S(1)} %get-tuple-element.90) | copy-start | bytes 3076
  15.0 13.5 %copy-start.25 = (f32[1,1,256]{2,1,0:T(1,128)}, f32[1,1,256]{2,1,0:T(1,128)S(1)}, u32[]{:S(2)}) copy-start(f32[1,1,256]{2,1,0:T(1,128)S(1)} %get-tuple-element.91) | copy-start | bytes 3076
  15.0 13.5 %copy-start.27 = (f32[1,1,256]{2,1,0:T(1,128)}, f32[1,1,256]{2,1,0:T(1,128)S(1)}, u32[]{:S(2)}) copy-start(f32[1,1,256]{2,1,0:T(1,128)S(1)} %get-tuple-element.92) | copy-start | bytes 3076
  15.0 13.5 %copy-start.29 = (f32[1,1,256]{2,1,0:T(1,128)}, f32[1,1,256]{2,1,0:T(1,128)S(1)}, u32[]{:S(2)}) copy-start(f32[1,1,256]{2,1,0:T(1,128)S(1)} %get-tuple-element.93) | copy-start | bytes 3076
  15.0 13.5 %copy-start.31 = (f32[1,1,256]{2,1,0:T(1,128)}, f32[1,1,256]{2,1,0:T(1,128)S(1)}, u32[]{:S(2)}) copy-start(f32[1,1,256]{2,1,0:T(1,128)S(1)} %get-tuple-element.94) | copy-start | bytes 3076
  15.0 13.5 %copy-start.33 = (f32[1,1,256]{2,1,0:T(1,128)}, f32[1,1,256]{2,1,0:T(1,128)S(1)}, u32[]{:S(2)}) copy-start(f32[1,1,256]{2,1,0:T(1,128)S(1)} %get-tuple-element.95) | copy-start | bytes 3076
  15.0 13.5 %copy-start.35 = (f32[1,1,256]{2,1,0:T(1,128)}, f32[1,1,256]{2,1,0:T(1,128)S(1)}, u32[]{:S(2)}) copy-start(f32[1,1,256]{2,1,0:T(1,128)S(1)} %get-tuple-element.96) | copy-start | bytes 3076
  15.0 13.5 %copy-start.37 = (f32[1,1,256]{2,1,0:T(1,128)}, f32[1,1,256]{2,1,0:T(1,128)S(1)}, u32[]{:S(2)}) copy-start(f32[1,1,256]{2,1,0:T(1,128)S(1)} %get-tuple-element.97) | copy-start | bytes 3076
  15.0 13.5 %copy-start.39 = (f32[1,1,256]{2,1,0:T(1,128)}, f32[1,1,256]{2,1,0:T(1,128)S(1)}, u32[]{:S(2)}) copy-start(f32[1,1,256]{2,1,0:T(1,128)S(1)} %get-tuple-element.98) | copy-start | bytes 3076
  15.0 13.5 %copy-start.41 = (f32[1,1,256]{2,1,0:T(1,128)}, f32[1,1,256]{2,1,0:T(1,128)S(1)}, u32[]{:S(2)}) copy-start(f32[1,1,256]{2,1,0:T(1,128)S(1)} %get-tuple-element.99) | copy-start | bytes 3076
  15.1 13.5 %copy-start.43 = (f32[1,1,256]{2,1,0:T(1,128)}, f32[1,1,256]{2,1,0:T(1,128)S(1)}, u32[]{:S(2)}) copy-start(f32[1,1,256]{2,1,0:T(1,128)S(1)} %get-tuple-element.100) | copy-start | bytes 3076
  15.1 13.5 %copy-start.45 = (f32[1,1,256]{2,1,0:T(1,128)}, f32[1,1,256]{2,1,0:T(1,128)S(1)}, u32[]{:S(2)}) copy-start(f32[1,1,256]{2,1,0:T(1,128)S(1)} %get-tuple-element.101) | copy-start | bytes 3076
  15.1 13.5 %copy-start.47 = (f32[1,1,256]{2,1,0:T(1,128)}, f32[1,1,256]{2,1,0:T(1,128)S(1)}, u32[]{:S(2)}) copy-start(f32[1,1,256]{2,1,0:T(1,128)S(1)} %get-tuple-element.102) | copy-start | bytes 3076
  15.1 13.1 %copy-start.4 = (bf16[1,32,16,256]{3,2,1,0:T(8,128)(2,1)S(1)}, bf16[1,32,16,256]{3,2,1,0:T(8,128)(2,1)}, u32[]{:S(2)}) copy-start(bf16[1,32,16,256]{3,2,1,0:T(8,128)(2,1)} %param.8) | copy-start | bytes 786436
  17.6 11.0 %copy-start.49 = (f32[1,1,256]{2,1,0:T(1,128)}, f32[1,1,256]{2,1,0:T(1,128)S(1)}, u32[]{:S(2)}) copy-start(f32[1,1,256]{2,1,0:T(1,128)S(1)} %get-tuple-element.103) | copy-start | bytes 3076
  17.6 11.0 %copy-start.51 = (f32[1,1,256]{2,1,0:T(1,128)}, f32[1,1,256]{2,1,0:T(1,128)S(1)}, u32[]{:S(2)}) copy-start(f32[1,1,256]{2,1,0:T(1,128)S(1)} %get-tuple-element.104) | copy-start | bytes 3076
  17.6 11.0 %copy-start.53 = (f32[1,1,256]{2,1,0:T(1,128)}, f32[1,1,256]{2,1,0:T(1,128)S(1)}, u32[]{:S(2)}) copy-start(f32[1,1,256]{2,1,0:T(1,128)S(1)} %get-tuple-element.105) | copy-start | bytes 3076
  17.6 11.0 %copy-start.55 = (f32[1,1,256]{2,1,0:T(1,128)}, f32[1,1,256]{2,1,0:T(1,128)S(1)}, u32[]{:S(2)}) copy-start(f32[1,1,256]{2,1,0:T(1,128)S(1)} %get-tuple-element.106) | copy-start | bytes 3076
  17.6 11.0 %copy-start.57 = (f32[1,1,256]{2,1,0:T(1,128)}, f32[1,1,256]{2,1,0:T(1,128)S(1)}, u32[]{:S(2)}) copy-start(f32[1,1,256]{2,1,0:T(1,128)S(1)} %get-tuple-element.107) | copy-start | bytes 3076
  17.6 11.0 %copy-start.59 = (f32[1,1,256]{2,1,0:T(1,128)}, f32[1,1,256]{2,1,0:T(1,128)S(1)}, u32[]{:S(2)}) copy-start(f32[1,1,256]{2,1,0:T(1,128)S(1)} %get-tuple-element.108) | copy-start | bytes 3076
  17.6 11.0 %copy-start.61 = (f32[1,1,256]{2,1,0:T(1,128)}, f32[1,1,256]{2,1,0:T(1,128)S(1)}, u32[]{:S(2)}) copy-start(f32[1,1,256]{2,1,0:T(1,128)S(1)} %get-tuple-element.109) | copy-start | bytes 3076
  17.6 11.0 %copy-start.63 = (f32[1,1,256]{2,1,0:T(1,128)}, f32[1,1,256]{2,1,0:T(1,128)S(1)}, u32[]{:S(2)}) copy-start(f32[1,1,256]{2,1,0:T(1,128)S(1)} %get-tuple-element.110) | copy-start | bytes 3076
  17.6 11.0 %copy-start.65 = (f32[1,1,256]{2,1,0:T(1,128)}, f32[1,1,256]{2,1,0:T(1,128)S(1)}, u32[]{:S(2)}) copy-start(f32[1,1,256]{2,1,0:T(1,128)S(1)} %get-tuple-element.111) | copy-start | bytes 3076
  17.6 11.0 %copy-start.67 = (f32[1,1,256]{2,1,0:T(1,128)}, f32[1,1,256]{2,1,0:T(1,128)S(1)}, u32[]{:S(2)}) copy-start(f32[1,1,256]{2,1,0:T(1,128)S(1)} %get-tuple-element.112) | copy-start | bytes 3076
  17.7 11.0 %copy-start.69 = (f32[1,1,256]{2,1,0:T(1,128)}, f32[1,1,256]{2,1,0:T(1,128)S(1)}, u32[]{:S(2)}) copy-start(f32[1,1,256]{2,1,0:T(1,128)S(1)} %get-tuple-element.113) | copy-start | bytes 3076
  17.7 11.0 %copy-start.71 = (f32[1,1,256]{2,1,0:T(1,128)}, f32[1,1,256]{2,1,0:T(1,128)S(1)}, u32[]{:S(2)}) copy-start(f32[1,1,256]{2,1,0:T(1,128)S(1)} %get-tuple-element.114) | copy-start | bytes 3076
  17.7 11.0 %copy-start.73 = (f32[1,1,256]{2,1,0:T(1,128)}, f32[1,1,256]{2,1,0:T(1,128)S(1)}, u32[]{:S(2)}) copy-start(f32[1,1,256]{2,1,0:T(1,128)S(1)} %get-tuple-element.115) | copy-start | bytes 3076
  17.7 11.0 %copy-start.75 = (f32[1,1,256]{2,1,0:T(1,128)}, f32[1,1,256]{2,1,0:T(1,128)S(1)}, u32[]{:S(2)}) copy-start(f32[1,1,256]{2,1,0:T(1,128)S(1)} %get-tuple-element.116) | copy-start | bytes 3076
  17.7 11.0 %copy-start.77 = (f32[1,1,256]{2,1,0:T(1,128)}, f32[1,1,256]{2,1,0:T(1,128)S(1)}, u32[]{:S(2)}) copy-start(f32[1,1,256]{2,1,0:T(1,128)S(1)} %get-tuple-element.117) | copy-start | bytes 3076
  17.7 11.0 %copy-start.79 = (f32[1,1,256]{2,1,0:T(1,128)}, f32[1,1,256]{2,1,0:T(1,128)S(1)}, u32[]{:S(2)}) copy-start(f32[1,1,256]{2,1,0:T(1,128)S(1)} %get-tuple-element.118) | copy-start | bytes 3076
  17.7 11.0 %copy-start.81 = (f32[1,1,256]{2,1,0:T(1,128)}, f32[1,1,256]{2,1,0:T(1,128)S(1)}, u32[]{:S(2)}) copy-start(f32[1,1,256]{2,1,0:T(1,128)S(1)} %get-tuple-element.119) | copy-start | bytes 3076
  17.7 11.0 %copy-start.83 = (f32[1,1,256]{2,1,0:T(1,128)}, f32[1,1,256]{2,1,0:T(1,128)S(1)}, u32[]{:S(2)}) copy-start(f32[1,1,256]{2,1,0:T(1,128)S(1)} %get-tuple-element.120) | copy-start | bytes 3076
  17.7 11.0 %copy-start.85 = (f32[1,1,256]{2,1,0:T(1,128)}, f32[1,1,256]{2,1,0:T(1,128)S(1)}, u32[]{:S(2)}) copy-start(f32[1,1,256]{2,1,0:T(1,128)S(1)} %get-tuple-element.121) | copy-start | bytes 3076
  18.6 8.4 %collective-permute-start.2 = (bf16[1,3,22,256]{3,2,1,0:T(8,128)(2,1)S(1)}, bf16[1,3,22,256]{3,2,1,0:T(8,128)(2,1)S(1)}, u32[]{:S(2)}, u32[]{:S(2)}) collective-permute-start(bf16[1,3,22,256]{3,2,1,0:T(8,128)(2,1)S(1)} %get-tuple-element.78), channel_id=1, source_target_pairs={{0,1},{2,3},{4,5},{6,7},{8,9},{10,11},{12,13},{14,15},{16,17},{18,... | collective-permute-start | bytes 101384 | tf_op jit(solution)/shard_map/ppermute | solution.py:20
  22.4 5.9 %collective-permute-start.3 = (bf16[1,3,22,256]{3,2,1,0:T(8,128)(2,1)S(1)}, bf16[1,3,22,256]{3,2,1,0:T(8,128)(2,1)S(1)}, u32[]{:S(2)}, u32[]{:S(2)}) collective-permute-start(bf16[1,3,22,256]{3,2,1,0:T(8,128)(2,1)S(1)} %get-tuple-element.79), channel_id=1, source_target_pairs={{1,0},{3,2},{5,4},{7,6},{9,8},{11,10},{13,12},{15,14},{17,16},{19,... | collective-permute-start | bytes 101384 | tf_op jit(solution)/shard_map/ppermute | solution.py:22
  45.7 203.8 %all-reduce.8.cloned.1.call-start = ((), (), s32[]{:S(2)}) async-start(), calls=%async_computation | async-start | bytes 4194304 | tf_op jit(solution)/shard_map/psum | solution.py:93
  58.7 291.3 %all-reduce.10.cloned.1.call-start = ((), (), s32[]{:S(2)}) async-start(), calls=%async_computation.1 | async-start | bytes 4194304 | tf_op jit(solution)/shard_map/psum | solution.py:162
  58.8 75.0 %collective-permute-start.4 = (bf16[1,32,3,256]{3,2,1,0:T(4,128)(2,1)S(1)}, bf16[1,32,3,256]{3,2,1,0:T(4,128)(2,1)S(1)}, u32[]{:S(2)}, u32[]{:S(2)}) collective-permute-start(bf16[1,32,3,256]{3,2,1,0:T(4,128)(2,1)S(1)} %get-tuple-element.80), channel_id=1, source_target_pairs={{0,2},{2,4},{4,6},{6,8},{8,10},{10,12},{12,14},{14,16},{16,18},{18... | collective-permute-start | bytes 147464 | tf_op jit(solution)/shard_map/ppermute | solution.py:20
  58.9 74.9 %collective-permute-start.5 = (bf16[1,32,3,256]{3,2,1,0:T(4,128)(2,1)S(1)}, bf16[1,32,3,256]{3,2,1,0:T(4,128)(2,1)S(1)}, u32[]{:S(2)}, u32[]{:S(2)}) collective-permute-start(bf16[1,32,3,256]{3,2,1,0:T(4,128)(2,1)S(1)} %get-tuple-element.81), channel_id=1, source_target_pairs={{2,0},{4,2},{6,4},{8,6},{10,8},{12,10},{14,12},{16,14},{18,16},{20... | collective-permute-start | bytes 147464 | tf_op jit(solution)/shard_map/ppermute | solution.py:22
  132.8 9.9 %copy-start.18 = (f32[1,1,256]{2,1,0:T(1,128)S(1)}, f32[1,1,256]{2,1,0:T(1,128)}, u32[]{:S(2)}) copy-start(f32[1,1,256]{2,1,0:T(1,128)} %copy-done.17) | copy-start | bytes 3076
  132.8 9.9 %copy-start.20 = (f32[1,1,256]{2,1,0:T(1,128)S(1)}, f32[1,1,256]{2,1,0:T(1,128)}, u32[]{:S(2)}) copy-start(f32[1,1,256]{2,1,0:T(1,128)} %copy-done.19) | copy-start | bytes 3076
  132.8 9.9 %copy-start.22 = (f32[1,1,256]{2,1,0:T(1,128)S(1)}, f32[1,1,256]{2,1,0:T(1,128)}, u32[]{:S(2)}) copy-start(f32[1,1,256]{2,1,0:T(1,128)} %copy-done.21) | copy-start | bytes 3076
  132.9 9.9 %copy-start.24 = (f32[1,1,256]{2,1,0:T(1,128)S(1)}, f32[1,1,256]{2,1,0:T(1,128)}, u32[]{:S(2)}) copy-start(f32[1,1,256]{2,1,0:T(1,128)} %copy-done.23) | copy-start | bytes 3076
  132.9 9.9 %copy-start.26 = (f32[1,1,256]{2,1,0:T(1,128)S(1)}, f32[1,1,256]{2,1,0:T(1,128)}, u32[]{:S(2)}) copy-start(f32[1,1,256]{2,1,0:T(1,128)} %copy-done.25) | copy-start | bytes 3076
  132.9 9.9 %copy-start.28 = (f32[1,1,256]{2,1,0:T(1,128)S(1)}, f32[1,1,256]{2,1,0:T(1,128)}, u32[]{:S(2)}) copy-start(f32[1,1,256]{2,1,0:T(1,128)} %copy-done.27) | copy-start | bytes 3076
  132.9 9.9 %copy-start.30 = (f32[1,1,256]{2,1,0:T(1,128)S(1)}, f32[1,1,256]{2,1,0:T(1,128)}, u32[]{:S(2)}) copy-start(f32[1,1,256]{2,1,0:T(1,128)} %copy-done.29) | copy-start | bytes 3076
  132.9 9.9 %copy-start.32 = (f32[1,1,256]{2,1,0:T(1,128)S(1)}, f32[1,1,256]{2,1,0:T(1,128)}, u32[]{:S(2)}) copy-start(f32[1,1,256]{2,1,0:T(1,128)} %copy-done.31) | copy-start | bytes 3076
  132.9 9.9 %copy-start.34 = (f32[1,1,256]{2,1,0:T(1,128)S(1)}, f32[1,1,256]{2,1,0:T(1,128)}, u32[]{:S(2)}) copy-start(f32[1,1,256]{2,1,0:T(1,128)} %copy-done.33) | copy-start | bytes 3076
  132.9 9.9 %copy-start.36 = (f32[1,1,256]{2,1,0:T(1,128)S(1)}, f32[1,1,256]{2,1,0:T(1,128)}, u32[]{:S(2)}) copy-start(f32[1,1,256]{2,1,0:T(1,128)} %copy-done.35) | copy-start | bytes 3076
  132.9 9.9 %copy-start.38 = (f32[1,1,256]{2,1,0:T(1,128)S(1)}, f32[1,1,256]{2,1,0:T(1,128)}, u32[]{:S(2)}) copy-start(f32[1,1,256]{2,1,0:T(1,128)} %copy-done.37) | copy-start | bytes 3076
  132.9 9.9 %copy-start.40 = (f32[1,1,256]{2,1,0:T(1,128)S(1)}, f32[1,1,256]{2,1,0:T(1,128)}, u32[]{:S(2)}) copy-start(f32[1,1,256]{2,1,0:T(1,128)} %copy-done.39) | copy-start | bytes 3076
  132.9 9.9 %copy-start.42 = (f32[1,1,256]{2,1,0:T(1,128)S(1)}, f32[1,1,256]{2,1,0:T(1,128)}, u32[]{:S(2)}) copy-start(f32[1,1,256]{2,1,0:T(1,128)} %copy-done.41) | copy-start | bytes 3076
  133.0 9.9 %copy-start.44 = (f32[1,1,256]{2,1,0:T(1,128)S(1)}, f32[1,1,256]{2,1,0:T(1,128)}, u32[]{:S(2)}) copy-start(f32[1,1,256]{2,1,0:T(1,128)} %copy-done.43) | copy-start | bytes 3076
  133.9 5.9 %collective-permute-start.6 = (bf16[1,3,22,256]{3,2,1,0:T(8,128)(2,1)S(1)}, bf16[1,3,22,256]{3,2,1,0:T(8,128)(2,1)S(1)}, u32[]{:S(2)}, u32[]{:S(2)}) collective-permute-start(bf16[1,3,22,256]{3,2,1,0:T(8,128)(2,1)S(1)} %get-tuple-element.76), channel_id=1, source_target_pairs={{0,1},{2,3},{4,5},{6,7},{8,9},{10,11},{12,13},{14,15},{16,17},{18,... | collective-permute-start | bytes 101384 | tf_op jit(solution)/shard_map/ppermute | solution.py:20
  136.6 5.9 %collective-permute-start.7 = (bf16[1,3,22,256]{3,2,1,0:T(8,128)(2,1)S(1)}, bf16[1,3,22,256]{3,2,1,0:T(8,128)(2,1)S(1)}, u32[]{:S(2)}, u32[]{:S(2)}) collective-permute-start(bf16[1,3,22,256]{3,2,1,0:T(8,128)(2,1)S(1)} %get-tuple-element.77), channel_id=1, source_target_pairs={{1,0},{3,2},{5,4},{7,6},{9,8},{11,10},{13,12},{15,14},{17,16},{19,... | collective-permute-start | bytes 101384 | tf_op jit(solution)/shard_map/ppermute | solution.py:22
  (62 other events, 360.3 us)
Sparse Core Ops, SparseCore 0:
  45.8 63.0 all-reduce.11
  115.7 133.7 all-reduce.7
  253.1 96.9 all-reduce.9
